TPU v7x, 32 devices: a whole 2x2x4 slice. The times are simulated.
32 devices in a mesh: dp: 8 (over z, x), shard: 4 (over y, core).
Axes of the slice: x: 2, y: 2, z: 4, core: 2. Of those that a mesh axis runs over, the one named last changes fastest.
Arguments:
- noisy: float32 [128, 256, 16], P(('dp', 'shard')), may hold values from -6 to 6
- velocity: float32 [128, 256, 16], P(('dp', 'shard')), may hold values from -6 to 6
- tstep_idx: int32 [128], P(('dp', 'shard')), may hold values from 0 to 999
- class_ids: int32 [128], P(('dp', 'shard')), may hold values from 0 to 1000
- time_weight: float32 [128], P(('dp', 'shard')), may hold values from 0.3 to 3
- dino: bfloat16 [128, 256, 768], P(('dp', 'shard')), may hold values from -6 to 6
- owner_map: int32 [12], replicated, may hold values from 0 to 11, each once
- adam_flat: float32 [2129920], P(('dp', 'shard')), may hold values from -4 to 4
- adam_m: float32 [2129920], P(('dp', 'shard')), may hold values from -0.015625 to 0.015625
- adam_v: float32 [2129920], P(('dp', 'shard')), may hold values from 1e-06 to 0.0001
- blocks_w: float32 [12, 384, 384], P('shard'), may hold values from -0.3125 to 0.3125
- stat_left: float32 [12, 384, 384], P('shard'), may hold values from -0.005 to 0.01, as said below
- stat_right: float32 [12, 384, 384], P('shard'), may hold values from -0.005 to 0.01, as said below
- root_left: float32 [12, 384, 384], P('shard'), may hold values from -3 to 3, as said below
- root_right: float32 [12, 384, 384], P('shard'), may hold values from -3 to 3, as said below
Outputs:
- loss: float32 [], replicated
- block_update: float32 [12, 384, 384], P('shard')
- stat_left_new: float32 [12, 384, 384], P('shard')
- stat_right_new: float32 [12, 384, 384], P('shard')
- adam_update: float32 [2129920], P(('dp', 'shard'))
- adam_m_new: float32 [2129920], P(('dp', 'shard'))
- adam_v_new: float32 [2129920], P(('dp', 'shard'))
Inputs may be any that keep to these rules, and one draw needn't show every extreme that they name: `owner_map`: each block number appears once. `stat_left`: each slot is symmetric positive definite. `stat_right`: each slot is symmetric positive definite. `root_left`: each slot is symmetric positive definite. `root_right`: each slot is symmetric positive definite.
All inputs are finite; a program needn't handle non-finite values.
Results may differ from a plain program's by a relative error of at most 0.0097.
Values may be sent and summed in bfloat16 or wider, within the bound.
No kernel may reach another device: no remote copies, remote signals or barrier semaphores. Data moves between devices by JAX's collectives and lax.ppermute only.
A program may use at most 192 MiB of HBM per device.

v0:
```python
import functools
import math
import jax
import jax.numpy as jnp
from jax import lax
from jax.sharding import PartitionSpec as P

D = 384
HEADS = 6
HDIM = 64
F = 1536
PD = 16
GRID = 16
SEQ = 256
FREQ = 256
NCLS = 1001
DINO = 768
STEP = 10
NBLK = 12
ADAM_LEN = 2125072
ADAM_PAD = 2129920
HIGHEST = lax.Precision.HIGHEST
BETA_ONE = 0.9
BETA_TWO = 0.95
ADAM_EPS = 1e-08
ADAM_RATE = 0.01
DECAY_RATE = 0.1
STAT_BETA = 0.9
SHAMPOO_RATE = 0.02
RMS_EPS = 1e-08
REPA_WEIGHT = 0.5
NORM_EPS = 1e-06


def segment_shapes():
    return [
        (PD, D),
        (D,),
        (FREQ, D),
        (D,),
        (D, D),
        (D,),
        (NCLS, D),
        (D, 6 * D),
        (6 * D,),
        (D,),
        (D,),
        (D,),
        (F,),
        (D,),
        (D, 2 * D),
        (2 * D,),
        (D, PD),
        (PD,),
        (D, DINO),
        (DINO,),
    ]


def unflatten(flat):
    pieces = []
    offset = 0
    for seg_dims in segment_shapes():
        length = math.prod(seg_dims)
        pieces.append(flat[offset : offset + length].reshape(seg_dims))
        offset += length
    return pieces


def position_table():
    quarter = D // 4
    frequencies = 1.0 / 10000.0 ** (jnp.arange(quarter, dtype=jnp.float32) / quarter)
    cell_ids = jnp.arange(SEQ, dtype=jnp.int32)
    row_arg = (cell_ids // GRID).astype(jnp.float32)[:, None] * frequencies[None, :]
    col_arg = (cell_ids % GRID).astype(jnp.float32)[:, None] * frequencies[None, :]
    return jnp.concatenate(
        [jnp.sin(col_arg), jnp.cos(col_arg), jnp.sin(row_arg), jnp.cos(row_arg)], axis=1
    )


def time_features(tstep_idx):
    half_freq = FREQ // 2
    frequencies = jnp.exp(-math.log(10000.0) * jnp.arange(half_freq, dtype=jnp.float32) / half_freq)
    angles = (tstep_idx.astype(jnp.float32) + 0.5)[:, None] * frequencies[None, :]
    return jnp.concatenate([jnp.cos(angles), jnp.sin(angles)], axis=1)


def normalize(values):
    centered = values - jnp.mean(values, axis=-1, keepdims=True)
    inv_dev = lax.rsqrt(jnp.mean(centered * centered, axis=-1, keepdims=True) + NORM_EPS)
    return (centered * inv_dev, inv_dev)


def normalize_back(grad_in, normed, inv_dev):
    return inv_dev * (
        grad_in
        - jnp.mean(grad_in, axis=-1, keepdims=True)
        - normed * jnp.mean(grad_in * normed, axis=-1, keepdims=True)
    )


def condition_terms(
    tstep_idx,
    class_ids,
    time_in_weight,
    time_in_bias,
    time_out_weight,
    time_out_bias,
    class_table,
    mod_weight,
    mod_bias,
    final_mod_weight,
    final_mod_bias,
):
    features = time_features(tstep_idx)
    time_hidden = jax.nn.silu(jnp.dot(features, time_in_weight, precision=HIGHEST) + time_in_bias)
    onehot_class = (class_ids[:, None] == jnp.arange(NCLS, dtype=jnp.int32)[None, :]).astype(
        jnp.float32
    )
    condition = (
        jnp.dot(time_hidden, time_out_weight, precision=HIGHEST)
        + time_out_bias
        + jnp.dot(onehot_class, class_table, precision=HIGHEST)
    )
    cond_act = jax.nn.silu(condition)
    modulation = jnp.dot(cond_act, mod_weight, precision=HIGHEST) + mod_bias
    final_mods = jnp.dot(cond_act, final_mod_weight, precision=HIGHEST) + final_mod_bias
    return (modulation, final_mods)


def cosine_total(aligned, dino_f):
    products = jnp.sum(aligned * dino_f, axis=-1)
    return jnp.sum(
        products
        * lax.rsqrt(jnp.sum(aligned * aligned, axis=-1) + NORM_EPS)
        * lax.rsqrt(jnp.sum(dino_f * dino_f, axis=-1) + NORM_EPS)
    )


def matmul(left, right):
    return jnp.dot(left, right, preferred_element_type=jnp.float32)


def row_total(rounded):
    return jnp.sum(rounded.astype(jnp.float32), axis=0)


def body(
    noisy,
    velocity,
    tstep_idx,
    class_ids,
    time_weight,
    dino,
    owner_map,
    adam_flat,
    adam_m,
    adam_v,
    blocks_w,
    stat_left,
    stat_right,
    root_left,
    root_right,
):
    devices = lax.axis_size("dp") * lax.axis_size("shard")
    images = noisy.shape[0]
    seq = noisy.shape[1]
    total_img = images * devices
    rows = images * seq
    fc_ratio = F // D
    flat_low = lax.all_gather(adam_flat.astype(jnp.bfloat16), ("dp", "shard"), axis=0, tiled=True)
    slot_low = lax.all_gather(blocks_w.astype(jnp.bfloat16), "shard", axis=0, tiled=True)
    block_ids = jnp.arange(NBLK, dtype=jnp.int32)
    slot_of = jnp.sum(
        block_ids[:, None] * (owner_map[:, None] == block_ids[None, :]).astype(jnp.int32), axis=0
    )
    blocks = jnp.take(slot_low, slot_of, axis=0)
    w_qkv = jnp.concatenate([blocks[0], blocks[1], blocks[2]], axis=1)
    w_proj = blocks[3]
    w_up = jnp.concatenate([blocks[4 + which] for which in range(fc_ratio)], axis=1)
    w_down = blocks[4 + fc_ratio :].reshape(F, D)
    pieces_low = unflatten(flat_low)
    pieces = [piece.astype(jnp.float32) for piece in pieces_low]
    (
        patch_weight,
        patch_bias,
        time_in_weight,
        time_in_bias,
        time_out_weight,
        time_out_bias,
        class_table,
        mod_weight,
        mod_bias,
        query_bias,
        value_bias,
        proj_bias,
        hidden_bias,
        down_bias,
        final_mod_weight,
        final_mod_bias,
        final_weight,
        final_bias,
        align_weight,
        align_bias,
    ) = pieces
    patch_low = pieces_low[0]
    final_low = pieces_low[16]
    align_low = pieces_low[18]
    cond_weights = (
        time_in_weight,
        time_in_bias,
        time_out_weight,
        time_out_bias,
        class_table,
        mod_weight,
        mod_bias,
        final_mod_weight,
        final_mod_bias,
    )
    (modulation, final_mods), cond_back = jax.vjp(
        functools.partial(condition_terms, tstep_idx, class_ids), *cond_weights
    )
    shift_one, scale_one, gate_one, shift_two, scale_two, gate_two = [
        modulation[:, None, which * D : (which + 1) * D] for which in range(6)
    ]
    final_shift = final_mods[:, None, :D]
    final_scale = final_mods[:, None, D:]
    noisy_low = noisy.astype(jnp.bfloat16).reshape(rows, PD)
    hidden0 = (matmul(noisy_low, patch_low) + patch_bias).reshape(images, seq, D) + position_table()
    norm_one, inv_one = normalize(hidden0)
    act_one = (norm_one * (1.0 + scale_one) + shift_one).astype(jnp.bfloat16).reshape(rows, D)
    qkv_bias = jnp.concatenate([query_bias, jnp.zeros((D,), jnp.float32), value_bias])
    projected = (
        (matmul(act_one, w_qkv) + qkv_bias)
        .astype(jnp.bfloat16)
        .reshape(images, seq, 3, HEADS, HDIM)
    )
    queries = projected[:, :, 0]
    key_part = projected[:, :, 1]
    values = projected[:, :, 2]
    scale_qk = HDIM ** (-0.5)
    scores = (
        jnp.einsum("gqhe,gkhe->ghqk", queries, key_part, preferred_element_type=jnp.float32)
        * scale_qk
    )
    row_max = jnp.max(scores, axis=-1, keepdims=True)
    log_total = row_max + jnp.log(jnp.sum(jnp.exp(scores - row_max), axis=-1, keepdims=True))
    probs_low = jnp.exp(scores - log_total).astype(jnp.bfloat16)
    attended = (
        jnp.einsum("ghqk,gkhe->gqhe", probs_low, values, preferred_element_type=jnp.float32)
        .reshape(rows, D)
        .astype(jnp.bfloat16)
    )
    branch_one = (matmul(attended, w_proj) + proj_bias).reshape(images, seq, D)
    hidden1 = hidden0 + gate_one * branch_one
    norm_two, inv_two = normalize(hidden1)
    act_two = (norm_two * (1.0 + scale_two) + shift_two).astype(jnp.bfloat16).reshape(rows, D)
    inner_pre = matmul(act_two, w_up) + hidden_bias
    gelu_out, gelu_back = jax.vjp(functools.partial(jax.nn.gelu, approximate=True), inner_pre)
    gelu_low = gelu_out.astype(jnp.bfloat16)
    branch_two = (matmul(gelu_low, w_down) + down_bias).reshape(images, seq, D)
    hidden2 = hidden1 + gate_two * branch_two
    norm_three, inv_three = normalize(hidden2)
    act_three = (
        (norm_three * (1.0 + final_scale) + final_shift).astype(jnp.bfloat16).reshape(rows, D)
    )
    output = (matmul(act_three, final_low) + final_bias).reshape(images, seq, PD)
    errors = output - velocity
    main_term = jnp.sum(time_weight[:, None, None] * errors * errors) / (total_img * SEQ * PD)
    hidden1_low = hidden1.astype(jnp.bfloat16).reshape(rows, D)
    aligned = matmul(hidden1_low, align_low) + align_bias
    dino_f = dino.astype(jnp.float32).reshape(rows, DINO)
    cosine_sum, cosine_back = jax.vjp(functools.partial(cosine_total, dino_f=dino_f), aligned)
    align_scale = REPA_WEIGHT / (total_img * SEQ)
    loss_local = main_term - align_scale * cosine_sum
    back_output = (
        (2.0 * time_weight[:, None, None] * errors / (total_img * SEQ * PD))
        .reshape(rows, PD)
        .astype(jnp.bfloat16)
    )
    grad_final = matmul(act_three.T, back_output)
    grad_final_bias = row_total(back_output)
    back_three = matmul(back_output, final_low.T).reshape(images, seq, D)
    grad_final_shift = jnp.sum(back_three, axis=1)
    grad_final_scale = jnp.sum(back_three * norm_three, axis=1)
    back_hidden2 = normalize_back(back_three * (1.0 + final_scale), norm_three, inv_three)
    back_branch_two = (back_hidden2 * gate_two).reshape(rows, D).astype(jnp.bfloat16)
    grad_gate_two = jnp.sum(back_hidden2 * branch_two, axis=1)
    grad_down = matmul(gelu_low.T, back_branch_two)
    grad_down_bias = row_total(back_branch_two)
    back_inner = gelu_back(matmul(back_branch_two, w_down.T))[0].astype(jnp.bfloat16)
    grad_up = matmul(act_two.T, back_inner)
    grad_hidden_bias = row_total(back_inner)
    back_two = matmul(back_inner, w_up.T).reshape(images, seq, D)
    grad_shift_two = jnp.sum(back_two, axis=1)
    grad_scale_two = jnp.sum(back_two * norm_two, axis=1)
    back_aligned = cosine_back(jnp.asarray(-align_scale, jnp.float32))[0].astype(jnp.bfloat16)
    grad_align = matmul(hidden1_low.T, back_aligned)
    grad_align_bias = row_total(back_aligned)
    back_hidden1 = (
        back_hidden2
        + normalize_back(back_two * (1.0 + scale_two), norm_two, inv_two)
        + matmul(back_aligned, align_low.T).reshape(images, seq, D)
    )
    back_branch_one = (back_hidden1 * gate_one).reshape(rows, D).astype(jnp.bfloat16)
    grad_gate_one = jnp.sum(back_hidden1 * branch_one, axis=1)
    grad_proj = matmul(attended.T, back_branch_one)
    grad_proj_bias = row_total(back_branch_one)
    back_attended = (
        matmul(back_branch_one, w_proj.T).astype(jnp.bfloat16).reshape(images, seq, HEADS, HDIM)
    )
    back_probs = jnp.einsum(
        "gqhe,gkhe->ghqk", back_attended, values, preferred_element_type=jnp.float32
    )
    grad_values = jnp.einsum(
        "ghqk,gqhe->gkhe", probs_low, back_attended, preferred_element_type=jnp.float32
    )
    scores_again = (
        jnp.einsum("gqhe,gkhe->ghqk", queries, key_part, preferred_element_type=jnp.float32)
        * scale_qk
    )
    probs_again = jnp.exp(scores_again - log_total)
    back_scores = (
        probs_again * (back_probs - jnp.sum(back_probs * probs_again, axis=-1, keepdims=True))
    ).astype(jnp.bfloat16)
    grad_queries = (
        jnp.einsum("ghqk,gkhe->gqhe", back_scores, key_part, preferred_element_type=jnp.float32)
        * scale_qk
    )
    grad_keys = (
        jnp.einsum("ghqk,gqhe->gkhe", back_scores, queries, preferred_element_type=jnp.float32)
        * scale_qk
    )
    back_projected = (
        jnp.stack([grad_queries, grad_keys, grad_values], axis=2)
        .reshape(rows, 3 * D)
        .astype(jnp.bfloat16)
    )
    grad_qkv = matmul(act_one.T, back_projected)
    grad_qkv_bias = row_total(back_projected)
    back_one = matmul(back_projected, w_qkv.T).reshape(images, seq, D)
    grad_shift_one = jnp.sum(back_one, axis=1)
    grad_scale_one = jnp.sum(back_one * norm_one, axis=1)
    back_hidden0 = (
        (back_hidden1 + normalize_back(back_one * (1.0 + scale_one), norm_one, inv_one))
        .reshape(rows, D)
        .astype(jnp.bfloat16)
    )
    grad_patch = matmul(noisy_low.T, back_hidden0)
    grad_patch_bias = row_total(back_hidden0)
    grad_modulation = jnp.concatenate(
        [
            grad_shift_one,
            grad_scale_one,
            grad_gate_one,
            grad_shift_two,
            grad_scale_two,
            grad_gate_two,
        ],
        axis=1,
    )
    grad_final_mods = jnp.concatenate([grad_final_shift, grad_final_scale], axis=1)
    cond_grads = cond_back((grad_modulation, grad_final_mods))
    grad_list = (
        [grad_patch, grad_patch_bias]
        + list(cond_grads[:7])
        + [
            grad_qkv_bias[:D],
            grad_qkv_bias[2 * D :],
            grad_proj_bias,
            grad_hidden_bias,
            grad_down_bias,
            cond_grads[7],
            cond_grads[8],
            grad_final,
            grad_final_bias,
            grad_align,
            grad_align_bias,
        ]
    )
    flat_grad = jnp.concatenate(
        [gradient_part.reshape(-1) for gradient_part in grad_list]
        + [jnp.zeros((ADAM_PAD - ADAM_LEN,), jnp.float32)]
    )
    grad_model = jnp.concatenate(
        [
            grad_qkv.reshape(D, 3, D).transpose(1, 0, 2),
            grad_proj[None],
            grad_up.reshape(D, fc_ratio, D).transpose(1, 0, 2),
            grad_down.reshape(fc_ratio, D, D),
        ],
        axis=0,
    )
    grad_slot = jnp.take(grad_model, owner_map, axis=0)
    flat_owned = lax.psum_scatter(flat_grad, ("dp", "shard"), scatter_dimension=0, tiled=True)
    loss_total = lax.psum(loss_local, ("dp", "shard"))
    summed = lax.psum(grad_slot, "dp")
    owned = lax.psum_scatter(
        summed.astype(jnp.bfloat16), "shard", scatter_dimension=0, tiled=True
    ).astype(jnp.float32)
    new_left = STAT_BETA * stat_left + (1.0 - STAT_BETA) * jnp.einsum(
        "bij,bkj->bik", owned, owned, precision=HIGHEST
    )
    new_right = STAT_BETA * stat_right + (1.0 - STAT_BETA) * jnp.einsum(
        "bji,bjk->bik", owned, owned, precision=HIGHEST
    )
    left_applied = jnp.einsum("bij,bjk->bik", root_left, owned, precision=HIGHEST)
    direction = jnp.einsum("bij,bjk->bik", left_applied, root_right, precision=HIGHEST)
    root_mean = jnp.sqrt(jnp.mean(direction * direction, axis=(1, 2), keepdims=True))
    block_update = -SHAMPOO_RATE * (direction / (root_mean + RMS_EPS) + DECAY_RATE * blocks_w)
    new_m = BETA_ONE * adam_m + (1.0 - BETA_ONE) * flat_owned
    new_v = BETA_TWO * adam_v + (1.0 - BETA_TWO) * flat_owned * flat_owned
    corrected_m = new_m / (1.0 - BETA_ONE**STEP)
    corrected_v = new_v / (1.0 - BETA_TWO**STEP)
    adam_update = -ADAM_RATE * (
        corrected_m / (jnp.sqrt(corrected_v) + ADAM_EPS) + DECAY_RATE * adam_flat
    )
    return (loss_total, block_update, new_left, new_right, adam_update, new_m, new_v)


def solution(mesh):
    return jax.shard_map(
        body,
        mesh=mesh,
        in_specs=(
            P(("dp", "shard"), None, None),
            P(("dp", "shard"), None, None),
            P(("dp", "shard")),
            P(("dp", "shard")),
            P(("dp", "shard")),
            P(("dp", "shard"), None, None),
            P(),
            P(("dp", "shard")),
            P(("dp", "shard")),
            P(("dp", "shard")),
            P("shard", None, None),
            P("shard", None, None),
            P("shard", None, None),
            P("shard", None, None),
            P("shard", None, None),
        ),
        out_specs=(
            P(),
            P("shard", None, None),
            P("shard", None, None),
            P("shard", None, None),
            P(("dp", "shard")),
            P(("dp", "shard")),
            P(("dp", "shard")),
        ),
        check_vma=False,
    )
```

profile of v0, /device:TPU:0, one launch (start us, length us, event | category | flops | bytes accessed | tf_op | source)
XLA Modules:
  0.0 797.5 jit_solution(3456417252762726016)
XLA Ops:
  17.3 26.3 %all-gather.5.cloned.1.call-done = bf16[12,384,384]{2,1,0:T(8,128)(2,1)} async-done(((bf16[3,384,384]{2,1,0:T(8,128)(2,1)}), bf16[12,384,384]{2,1,0:T(8,128)(2,1)}) %all-gather.5.cloned.1.call-update) | async-done | bytes 3538960 | tf_op jit(solution)/shard_map/all_gather | solution.py:172
  43.6 5.1 gather_fusion
  54.7 54.4 %all-gather.3.cloned.1.call-done = bf16[2129920]{0:T(1024)(128)(2,1)} async-done(((bf16[66560]{0:T(1024)(128)(2,1)}), bf16[2129920]{0:T(1024)(128)(2,1)}) %all-gather.3.cloned.1.call-update) | async-done | bytes 4259856 | tf_op jit(solution)/shard_map/all_gather | solution.py:171
  140.5 4.3 copy.90
  144.9 6.1 reshape.436
  159.4 3.6 fusion.106
  169.8 3.8 fusion.104
  188.0 7.3 fusion.13
  195.3 5.1 convert_reduce_fusion
  203.7 3.5 multiply_reduce_fusion.2
  221.7 7.7 multiply_reduce_fusion
  229.4 6.3 multiply_convert_fusion
  252.4 4.8 fusion.95
  276.5 4.7 reshape.451
  300.5 87.2 %concatenate.35 = f32[2129920]{0:T(1024)} concatenate(f32[6144]{0:T(1024)} %reshape.447, f32[384]{0:T(512)} %get-tuple-element.39, f32[98304]{0:T(1024)S(1)} %copy-done.57, f32[384]{0:T(512)} %get-tuple-element.37, f32[147456]{0:T(1024)S(1)} %reshape.449, f32[384]{0:T(512)} %get-tuple-element.110, f32[384384]{0:T(1024)} %reshape.450, f32[884736]{0:T(1024)} %reshape.451, ...), dimensions={0} | concatenate | bytes 17039360 | tf_op jit(solution)/shard_map/concatenate | solution.py:381
  391.3 4.9 copy.131
  396.2 5.1 convolution_bitcast_fusion
  401.3 4.7 copy.132
  406.1 4.2 fusion.114
  413.5 7.0 gather_fusion.1
  420.6 6.6 broadcast_select_fusion
  427.1 306.0 %all-reduce.5 = bf16[12,384,384]{2,1,0:T(8,128)(2,1)} all-reduce(f32[12,384,384]{2,1,0:T(8,128)} %broadcast_select_fusion), channel_id=1, replica_groups=mesh['dp'=8,'shard'=4] {'dp'}, use_global_device_ids=true, to_apply=%region_20.21 | all-reduce | flops 1769472 | bytes 10616832 | tf_op jit(solution)/shard_map/psum | solution.py:397
  734.7 40.7 %psum.14 = f32[]{:T(128)} all-reduce(f32[]{:T(128)S(6)} %sub.143), channel_id=1, replica_groups=mesh['dp'=8,'shard'=4] {'dp','shard'}, use_global_device_ids=true, to_apply=%region_14.15 | all-reduce | flops 1 | bytes 8 | tf_op jit(solution)/shard_map/psum | solution.py:396
  780.6 3.8 multiply_reduce_fusion.3
  (368 shorter events, 167.8 us)
Async XLA Ops:
  7.2 773.4 %copy-start = (f32[3,384,384]{2,1,0:T(8,128)S(1)}, f32[3,384,384]{2,1,0:T(8,128)}, u32[]{:S(2)}) copy-start(f32[3,384,384]{2,1,0:T(8,128)} %param.29) | copy-start | bytes 5308420
  7.2 36.4 %all-gather.5.cloned.1.call-start = ((), (), s32[]{:S(2)}) async-start(), calls=%async_computation.2 | async-start | bytes 4423680 | tf_op jit(solution)/shard_map/all_gather | solution.py:172
  9.9 99.2 %all-gather.3.cloned.1.call-start = ((), (), s32[]{:S(2)}) async-start(), calls=%async_computation.1 | async-start | bytes 4392960 | tf_op jit(solution)/shard_map/all_gather | solution.py:171
  11.6 763.7 %all-reduce.4.cloned.1.call-start = ((), (), s32[]{:S(2)}) async-start(), calls=%async_computation.4 | async-start | bytes 17039360
  17.3 114.4 %copy-start.88 = (f32[4,128]{1,0:T(4,128)}, f32[4,128]{1,0:T(4,128)S(1)}, u32[]{:S(2)}) copy-start(f32[4,128]{1,0:T(4,128)S(1)} %get-tuple-element.90) | copy-start | bytes 6148
  17.3 114.4 %copy-start.90 = (f32[4,128]{1,0:T(4,128)}, f32[4,128]{1,0:T(4,128)S(1)}, u32[]{:S(2)}) copy-start(f32[4,128]{1,0:T(4,128)S(1)} %get-tuple-element.91) | copy-start | bytes 6148
  169.8 6.8 copy-start.82
  180.8 7.1 slice-start.2
  182.8 5.2 slice-start.3
  188.0 7.3 copy-start.66
  195.3 5.1 copy-start.59
  221.7 17.5 %slice-start = ((s8[6291456]{0:T(1024)(128)(4,1)}), s8[4194304]{0:T(1024)(128)(4,1)S(1)}, s32[]{:S(2)}) async-start(s8[6291456]{0:T(1024)(128)(4,1)} %bitcast.283), calls=%async_computation.5 | async-start | bytes 8388608
  229.4 6.4 copy-start.26
  229.4 9.8 %slice-start.1 = ((s8[6291456]{0:T(1024)(128)(4,1)}), s8[2097152]{0:T(1024)(128)(4,1)S(1)}, s32[]{:S(2)}) async-start(s8[6291456]{0:T(1024)(128)(4,1)} %bitcast.283), calls=%async_computation.6 | async-start | bytes 4194304
  252.4 5.3 copy-start.18
  257.7 6.1 copy-start.50
  257.7 7.7 copy-start.4
  265.5 6.2 copy-start.16
  282.4 8.4 %copy-start.38 = (f32[384,768]{1,0:T(8,128)S(1)}, f32[384,768]{1,0:T(8,128)}, u32[]{:S(2)}) copy-start(f32[384,768]{1,0:T(8,128)} %fusion.46) | copy-start | bytes 3538948
  291.9 6.4 copy-start.33
  291.9 8.6 %copy-start.57 = (f32[98304]{0:T(1024)S(1)}, f32[98304]{0:T(1024)}, u32[]{:S(2)}) copy-start(f32[98304]{0:T(1024)} %reshape.448) | copy-start | bytes 1179652
  387.7 389.8 %reduce-scatter.2.cloned.1.call-start = ((), (), s32[]{:S(2)}) async-start(), calls=%async_computation.3 | async-start | bytes 4423680 | tf_op jit(solution)/shard_map/reduce_scatter | solution.py:398
  413.5 7.0 copy-start.95
  733.2 44.4 %copy-start.54 = (f32[3,384,384]{2,1,0:T(8,128)S(1)}, f32[3,384,384]{2,1,0:T(8,128)}, u32[]{:S(2)}) copy-start(f32[3,384,384]{2,1,0:T(8,128)} %param.28) | copy-start | bytes 5308420
  (83 other events, 246.4 us)
Sparse Core Ops, SparseCore 0:
  10.1 33.4 all-gather.4
  47.1 61.9 all-gather.2
  387.8 243.0 all-reduce.3
  733.3 39.5 reduce-scatter.1
where the time goes:
time: 810 us; the launch traced here: 798 us
  blocking collectives  347 us (43%)
  local copies, waits for them, and re-layouts  186 us (23%)
  matrix products  103 us (13%)
  waiting for transfers between devices  80.8 us (10%)
  other arithmetic  64.9 us (8%)
  between operations  16.6 us (2%)
    psum x1, blocking collectives, body(): summed = lax.psum(grad_slot, 'dp')  306 us
    concatenate x1, local copies, waits for them, and re-layouts, body(): jnp.concatenate([gradient_part.reshape(-1) for gradient_part in grad_list...  87.2 us
    dot_general x20, matrix products, matmul(): return jnp.dot(left, right, preferred_element_type=jnp.float32)  57.1 us
    all_gather x1, waiting for transfers between devices, body(): lax.all_gather(adam_flat.astype(jnp.bfloat16), ('dp', 'shard'), axis=0, t...  54.4 us
    psum x1, blocking collectives, body(): loss_total = lax.psum(loss_local, ('dp', 'shard'))  40.7 us
    all_gather x1, waiting for transfers between devices, body(): lax.all_gather(blocks_w.astype(jnp.bfloat16), 'shard', axis=0, tiled=True)  26.3 us
  transfers between devices with their start and end apart: 4, of which 2 were waited for; matrix products, arithmetic and copies ran while one was open for 7% of the time, Pallas kernels for 0%

commit v1 on v0

--- a/solution.py
+++ b/solution.py
@@ -30,6 +30,19 @@
 RMS_EPS = 1e-08
 REPA_WEIGHT = 0.5
 NORM_EPS = 1e-06
+
+
+def layers_all_recast(packet, net_axis):
+    sides = lax.axis_size(net_axis)
+    top, val2 = (packet, 0)
+    while 1 << val2 < sides:
+        m_next = lax.ppermute(top, net_axis, [(no, no ^ 1 << val2) for no in range(sides)])
+        top = top + m_next
+        val2 = val2 + 1
+    return top
+
+
+_spread_ratios = functools.partial(layers_all_recast, net_axis="dp")
 
 
 def segment_shapes():
@@ -394,7 +407,7 @@
     grad_slot = jnp.take(grad_model, owner_map, axis=0)
     flat_owned = lax.psum_scatter(flat_grad, ("dp", "shard"), scatter_dimension=0, tiled=True)
     loss_total = lax.psum(loss_local, ("dp", "shard"))
-    summed = lax.psum(grad_slot, "dp")
+    summed = _spread_ratios(grad_slot)
     owned = lax.psum_scatter(
         summed.astype(jnp.bfloat16), "shard", scatter_dimension=0, tiled=True
     ).astype(jnp.float32)

time: 810 us -> 1140 us (1.41)
  waiting for transfers between devices: 80.8 us -> 702 us
  blocking collectives: 347 us -> 37.2 us
  other arithmetic: 64.9 us -> 80.5 us
    ppermute x0 -> x3, waiting for transfers between devices: none -> 516 us  [layers_all_recast(): lax.ppermute(top, net_axis, [(no, no ^ 1 << val2) for no in range(sides)])]
    psum x1 -> x0, blocking collectives: 306 us -> none  [body(): summed = lax.psum(grad_slot, 'dp')]
    unnamed x5, waiting for transfers between devices: 0.07 us -> 64.4 us
    reduce_scatter x1, waiting for transfers between devices: 0.01 us -> 40.7 us  [body(): lax.psum_scatter(summed.astype(jnp.bfloat16), 'shard', scatter_dimension=...]
    add x0 -> x2, other arithmetic: none -> 13.2 us  [layers_all_recast(): top = top + m_next]
  transfers between devices with their start and end apart: 4 -> 7, of which waited for: 2 -> 7; matrix products, arithmetic and copies ran while one was open for 7% -> 15% of each run, Pallas kernels for 0% -> 0%
where the time goes in v1:
time: 1140 us; the launch traced here: 1130 us
  waiting for transfers between devices  702 us (62%)
  local copies, waits for them, and re-layouts  185 us (16%)
  matrix products  103 us (9%)
  other arithmetic  80.5 us (7%)
  blocking collectives  37.2 us (3%)
  between operations  16.8 us (1%)
    ppermute x3, waiting for transfers between devices, layers_all_recast(): lax.ppermute(top, net_axis, [(no, no ^ 1 << val2) for no in range(sides)])  516 us
    concatenate x1, local copies, waits for them, and re-layouts, body(): jnp.concatenate([gradient_part.reshape(-1) for gradient_part in grad_list...  87.1 us
    unnamed x5, waiting for transfers between devices  64.4 us
    dot_general x20, matrix products, matmul(): return jnp.dot(left, right, preferred_element_type=jnp.float32)  59.6 us
    all_gather x1, waiting for transfers between devices, body(): lax.all_gather(adam_flat.astype(jnp.bfloat16), ('dp', 'shard'), axis=0, t...  54.3 us
    reduce_scatter x1, waiting for transfers between devices, body(): lax.psum_scatter(summed.astype(jnp.bfloat16), 'shard', scatter_dimension=...  40.7 us
    psum x1, blocking collectives, body(): loss_total = lax.psum(loss_local, ('dp', 'shard'))  37.2 us
    all_gather x1, waiting for transfers between devices, body(): lax.all_gather(blocks_w.astype(jnp.bfloat16), 'shard', axis=0, tiled=True)  26.3 us
  transfers between devices with their start and end apart: 7, of which 7 were waited for; matrix products, arithmetic and copies ran while one was open for 15% of the time, Pallas kernels for 0%

profile of v1, /device:TPU:0, one launch (start us, length us, event | category | flops | bytes accessed | tf_op | source)
XLA Modules:
  0.0 1129.1 jit_solution(8352932541695347337)
XLA Ops:
  17.3 26.3 %all-gather.5.cloned.1.call-done = bf16[12,384,384]{2,1,0:T(8,128)(2,1)} async-done(((bf16[3,384,384]{2,1,0:T(8,128)(2,1)}), bf16[12,384,384]{2,1,0:T(8,128)(2,1)}) %all-gather.5.cloned.1.call-update) | async-done | bytes 3538960 | tf_op jit(solution)/shard_map/all_gather | solution.py:185
  43.6 5.1 gather_fusion
  54.8 54.3 %all-gather.3.cloned.1.call-done = bf16[2129920]{0:T(1024)(128)(2,1)} async-done(((bf16[66560]{0:T(1024)(128)(2,1)}), bf16[2129920]{0:T(1024)(128)(2,1)}) %all-gather.3.cloned.1.call-update) | async-done | bytes 4259856 | tf_op jit(solution)/shard_map/all_gather | solution.py:184
  144.9 6.1 reshape.436
  186.2 7.4 fusion.13
  193.6 5.1 convert_reduce_fusion
  220.6 7.5 multiply_reduce_fusion
  228.1 6.5 multiply_convert_fusion
  246.3 5.0 copy.131
  251.3 5.0 convolution_bitcast_fusion
  256.3 4.6 copy.132
  268.2 7.0 gather_fusion.1
  280.5 153.2 %collective-permute-done = f32[12,384,384]{2,1,0:T(8,128)} collective-permute-done((f32[12,384,384]{2,1,0:T(8,128)S(1)}, f32[12,384,384]{2,1,0:T(8,128)}, u32[]{:S(2)}, u32[]{:S(2)}) %collective-permute-start) | collective-permute-done | bytes 7077920 | tf_op jit(solution)/shard_map/ppermute | solution.py:39
  433.7 6.7 fusion.168
  451.0 143.3 %collective-permute-done.1 = f32[12,384,384]{2,1,0:T(8,128)} collective-permute-done((f32[12,384,384]{2,1,0:T(8,128)}, f32[12,384,384]{2,1,0:T(8,128)}, u32[]{:S(2)}, u32[]{:S(2)}) %collective-permute-start.1) | collective-permute-done | bytes 7077920 | tf_op jit(solution)/shard_map/ppermute | solution.py:39
  594.3 6.5 add.422
  603.3 4.8 fusion.95
  608.2 4.8 reshape.451
  648.5 87.1 %concatenate.35 = f32[2129920]{0:T(1024)} concatenate(f32[6144]{0:T(1024)} %reshape.447, f32[384]{0:T(512)} %get-tuple-element.39, f32[98304]{0:T(1024)S(1)} %copy-done.56, f32[384]{0:T(512)} %get-tuple-element.37, f32[147456]{0:T(1024)S(1)} %copy-done.49, f32[384]{0:T(512)} %get-tuple-element.110, f32[384384]{0:T(1024)} %reshape.450, f32[884736]{0:T(1024)} %reshape.451, ...), dimensions={0} | concatenate | bytes 17039360 | tf_op jit(solution)/shard_map/concatenate | solution.py:394
  735.9 219.5 %collective-permute-done.2 = f32[12,384,384]{2,1,0:T(8,128)} collective-permute-done((f32[12,384,384]{2,1,0:T(8,128)}, f32[12,384,384]{2,1,0:T(8,128)}, u32[]{:S(2)}, u32[]{:S(2)}) %collective-permute-start.2) | collective-permute-done | bytes 7077920 | tf_op jit(solution)/shard_map/ppermute | solution.py:39
  955.4 7.7 add_convert_fusion
  964.6 37.2 %psum.7 = f32[]{:T(128)} all-reduce(f32[]{:T(128)S(6)} %sub.143), channel_id=1, replica_groups=mesh['dp'=8,'shard'=4] {'dp','shard'}, use_global_device_ids=true, to_apply=%region_14.15 | all-reduce | flops 1 | bytes 8 | tf_op jit(solution)/shard_map/psum | solution.py:409
  1001.9 64.4 %all-reduce.3.cloned.1.call-done = f32[2129920]{0:T(1024)} async-done(((f32[2129920]{0:T(1024)}), f32[2129920]{0:T(1024)}) %all-reduce.3.cloned.1.call-update) | async-done | bytes 8519696
  1068.4 40.7 %reduce-scatter.2.cloned.1.call-done = bf16[3,384,384]{2,1,0:T(8,128)(2,1)} async-done(((bf16[12,384,384]{2,1,0:T(8,128)(2,1)}), bf16[3,384,384]{2,1,0:T(8,128)(2,1)}) %reduce-scatter.2.cloned.1.call-update) | async-done | bytes 884752 | tf_op jit(solution)/shard_map/reduce_scatter | solution.py:411
  (395 shorter events, 196.4 us)
Async XLA Ops:
  7.2 1105.0 %copy-start = (f32[3,384,384]{2,1,0:T(8,128)S(1)}, f32[3,384,384]{2,1,0:T(8,128)}, u32[]{:S(2)}) copy-start(f32[3,384,384]{2,1,0:T(8,128)} %param.29) | copy-start | bytes 5308420
  7.2 36.4 %all-gather.5.cloned.1.call-start = ((), (), s32[]{:S(2)}) async-start(), calls=%async_computation.2 | async-start | bytes 4423680 | tf_op jit(solution)/shard_map/all_gather | solution.py:185
  9.9 99.2 %all-gather.3.cloned.1.call-start = ((), (), s32[]{:S(2)}) async-start(), calls=%async_computation.1 | async-start | bytes 4392960 | tf_op jit(solution)/shard_map/all_gather | solution.py:184
  11.6 1054.6 %all-reduce.3.cloned.1.call-start = ((), (), s32[]{:S(2)}) async-start(), calls=%async_computation.4 | async-start | bytes 17039360
  17.3 114.3 %copy-start.94 = (f32[4,128]{1,0:T(4,128)}, f32[4,128]{1,0:T(4,128)S(1)}, u32[]{:S(2)}) copy-start(f32[4,128]{1,0:T(4,128)S(1)} %get-tuple-element.90) | copy-start | bytes 6148
  17.3 114.3 %copy-start.96 = (f32[4,128]{1,0:T(4,128)}, f32[4,128]{1,0:T(4,128)S(1)}, u32[]{:S(2)}) copy-start(f32[4,128]{1,0:T(4,128)S(1)} %get-tuple-element.91) | copy-start | bytes 6148
  136.3 28.6 %copy-start.83 = (f32[4,384]{1,0:T(4,128)}, f32[4,384]{1,0:T(4,128)S(1)}, u32[]{:S(2)}) copy-start(f32[4,384]{1,0:T(4,128)S(1)} %get-tuple-element.117) | copy-start | bytes 18436
  164.8 42.6 %copy-start.89 = (f32[4,256]{1,0:T(4,128)}, f32[4,256]{1,0:T(4,128)S(1)}, u32[]{:S(2)}) copy-start(f32[4,256]{1,0:T(4,128)S(1)} %rsqrt.60) | copy-start | bytes 12292
  220.6 16.3 %slice-start = ((s8[6291456]{0:T(1024)(128)(4,1)}), s8[4194304]{0:T(1024)(128)(4,1)S(1)}, s32[]{:S(2)}) async-start(s8[6291456]{0:T(1024)(128)(4,1)} %bitcast.283), calls=%async_computation.5 | async-start | bytes 8388608
  275.2 158.5 %copy-start.5 = (f32[12,384,384]{2,1,0:T(8,128)S(1)}, f32[12,384,384]{2,1,0:T(8,128)}, u32[]{:S(2)}) copy-start(f32[12,384,384]{2,1,0:T(8,128)} %gather_fusion.1) | copy-start | bytes 21233668
  279.0 162.7 %copy-start.17 = (bf16[4,256,3,6,64]{1,4,3,0,2:T(8,128)(2,1)S(1)}, bf16[4,256,3,6,64]{1,4,3,0,2:T(8,128)(2,1)}, u32[]{:S(2)}) copy-start(bf16[4,256,3,6,64]{1,4,3,0,2:T(8,128)(2,1)} %copy-done.16) | copy-start | bytes 7077892
  279.0 154.7 %collective-permute-start = (f32[12,384,384]{2,1,0:T(8,128)S(1)}, f32[12,384,384]{2,1,0:T(8,128)}, u32[]{:S(2)}, u32[]{:S(2)}) collective-permute-start(f32[12,384,384]{2,1,0:T(8,128)S(1)} %broadcast_select_fusion), channel_id=1, source_target_pairs={{0,4},{4,0},{8,12},{12,8},{16,20},{20,16},{24,28},{28,24},{1,5},{5... | collective-permute-start | bytes 21233672 | tf_op jit(solution)/shard_map/ppermute | solution.py:39
  440.3 154.0 %collective-permute-start.1 = (f32[12,384,384]{2,1,0:T(8,128)}, f32[12,384,384]{2,1,0:T(8,128)}, u32[]{:S(2)}, u32[]{:S(2)}) collective-permute-start(f32[12,384,384]{2,1,0:T(8,128)} %fusion.168), channel_id=1, source_target_pairs={{0,8},{4,12},{8,0},{12,4},{16,24},{20,28},{24,16},{28,20},{1,9},{5... | collective-permute-start | bytes 21233672 | tf_op jit(solution)/shard_map/ppermute | solution.py:39
  443.3 151.0 %slice-start.2 = ((s8[7077888]{0:T(1024)(128)(4,1)}), s8[4194304]{0:T(1024)(128)(4,1)S(1)}, s32[]{:S(2)}) async-start(s8[7077888]{0:T(1024)(128)(4,1)} %bitcast.288), calls=%async_computation.7 | async-start | bytes 8388608
  447.9 146.4 %slice-start.3 = ((s8[7077888]{0:T(1024)(128)(4,1)}), s8[2883584]{0:T(1024)(128)(4,1)S(1)}, s32[]{:S(2)}) async-start(s8[7077888]{0:T(1024)(128)(4,1)} %bitcast.288), calls=%async_computation.8 | async-start | bytes 5767168
  451.0 151.5 %copy-start.21 = (f32[1024,384]{1,0:T(8,128)S(1)}, f32[1024,384]{1,0:T(8,128)}, u32[]{:S(2)}) copy-start(f32[1024,384]{1,0:T(8,128)} %get-tuple-element.99) | copy-start | bytes 4718596
  451.0 151.5 %copy-start.23 = (f32[4,256,384]{2,1,0:T(8,128)S(1)}, f32[4,256,384]{2,1,0:T(8,128)}, u32[]{:S(2)}) copy-start(f32[4,256,384]{2,1,0:T(8,128)} %get-tuple-element.30) | copy-start | bytes 4718596
  600.9 354.6 %collective-permute-start.2 = (f32[12,384,384]{2,1,0:T(8,128)}, f32[12,384,384]{2,1,0:T(8,128)}, u32[]{:S(2)}, u32[]{:S(2)}) collective-permute-start(f32[12,384,384]{2,1,0:T(8,128)} %add.422), channel_id=1, source_target_pairs={{0,16},{4,20},{8,24},{12,28},{16,0},{20,4},{24,8},{28,12},{1,17},{... | collective-permute-start | bytes 21233672 | tf_op jit(solution)/shard_map/ppermute | solution.py:39
  637.0 9.3 copy-start.35
  639.2 9.3 copy-start.78
  639.2 9.3 copy-start.49
  639.2 9.3 copy-start.56
  735.7 373.5 %reduce-scatter.2.cloned.1.call-start = ((), (), s32[]{:S(2)}) async-start(), calls=%async_computation.3 | async-start | bytes 4423680 | tf_op jit(solution)/shard_map/reduce_scatter | solution.py:411
  963.2 146.0 %copy-start.52 = (f32[3,384,384]{2,1,0:T(8,128)S(1)}, f32[3,384,384]{2,1,0:T(8,128)}, u32[]{:S(2)}) copy-start(f32[3,384,384]{2,1,0:T(8,128)} %param.28) | copy-start | bytes 5308420
  (95 other events, 338.0 us)
Sparse Core Ops, SparseCore 0:
  10.1 33.4 all-gather.4
  47.1 61.9 all-gather.2
  735.8 330.4 all-reduce.2
  1068.7 40.4 reduce-scatter.1
